TPU v7x, 32 devices: a whole 2x2x4 slice. The times are simulated.
32 devices in a mesh: cache: 8 (over z, x), owner: 4 (over y, core).
Axes of the slice: x: 2, y: 2, z: 4, core: 2. Of those that a mesh axis runs over, the one named last changes fastest.
Arguments:
- cache: bfloat16 [32, 4, 128, 256], P('cache'), may hold values from -2.5 to 2.5
- backing: bfloat16 [32, 32, 128, 256], P('cache', 'owner'), may hold values from -2.5 to 2.5
- resident: int32 [32, 4], P('cache'), may hold values from 0 to 31, as said below
- promote: int32 [32, 2], P('cache'), may hold values from 0 to 31, as said below
- victim: int32 [32, 2], P('cache'), may hold values from 0 to 3, as said below
- lookups: int32 [2, 4096, 32, 8], P(None, 'owner', 'cache'), may hold values from 0 to 511
- route: int32 [2, 4, 1024], P(None, 'owner'), may hold values from 0 to 1023, each once within a row
- dcn_down: bfloat16 [8192, 128], P('cache'), may hold values from -0.0625 to 0.0625
- dcn_up: bfloat16 [128, 8192], P(None, 'cache'), may hold values from -0.5 to 0.5
- dcn_bias: float32 [8192], replicated, may hold values from -5 to 5
- mlp_in: bfloat16 [8192, 1024], P('cache'), may hold values from -0.0625 to 0.0625
- mlp_bias: float32 [1024], replicated, may hold values from -3 to 3
- mlp_out: float32 [1024], replicated, may hold values from -0.1875 to 0.1875
- out_bias: float32 [1], replicated, may hold values from -4 to 4
Outputs:
- scores: float32 [2, 4, 1024], P(None, 'owner', 'cache')
- new_cache: bfloat16 [32, 4, 128, 256], P('cache')
- new_backing: bfloat16 [32, 32, 128, 256], P('cache', 'owner')
Inputs may be any that keep to these rules, and one draw needn't show every extreme that they name: `resident`: for each feature, 4 distinct backing blocks. `promote`: for each feature, 2 distinct backing blocks, none of them in that feature's resident; block k belongs to owner k // 8. `victim`: for each feature, 2 distinct slots. `route`: each batch and owner group holds every request index once.
All inputs are finite; a program needn't handle non-finite values.
Results may differ from a plain program's by a relative error of at most 0.004.
Values may be sent and summed in bfloat16 or wider, within the bound.
A program may use at most 128 MiB of HBM per device.

v0:
```python
import jax
import jax.numpy as jnp
from jax import lax
from jax.sharding import PartitionSpec as P


def take_rows(table, wanted):
    return jax.vmap(lambda rows, chosen: rows[chosen])(table, wanted)


def pool_batch(requests, order, table):
    requests = requests[order]
    count = requests.shape[0]
    step = min(512, count)
    codes = jnp.arange(table.shape[1], dtype=jnp.int32)

    def one_block(lookup_block):
        counts = jnp.sum((lookup_block[..., None] == codes).astype(jnp.bfloat16), axis=2)
        return jnp.einsum("rfk,fke->rfe", counts, table, preferred_element_type=jnp.float32).astype(
            jnp.bfloat16
        )

    blocks = requests.reshape((count // step, step) + requests.shape[1:])
    pooled = lax.map(one_block, blocks)
    return pooled.reshape((count,) + pooled.shape[2:])


def on_device(
    cache,
    backing,
    resident,
    promote,
    victim,
    lookups,
    route,
    dcn_down,
    dcn_up,
    dcn_bias,
    mlp_in,
    mlp_bias,
    mlp_out,
    out_bias,
):
    held = cache.shape[0]
    slots = cache.shape[1]
    block = cache.shape[2]
    width = cache.shape[3]
    own_blocks = backing.shape[1]
    promoted_count = promote.shape[1]
    owner_here = lax.axis_index("owner")
    local_index = promote - owner_here * own_blocks
    owned_here = (local_index >= 0) & (local_index < own_blocks)
    clamped = jnp.clip(local_index, 0, own_blocks - 1)
    fetched = take_rows(backing, clamped)
    outgoing = jnp.where(owned_here[:, :, None, None], fetched, jnp.zeros_like(fetched))
    arrived = lax.all_gather(outgoing, "owner", axis=0, tiled=True)
    owners = arrived.shape[0] // held
    arrived = arrived.reshape(owners, held, promoted_count, block, width)
    source = promote // own_blocks
    picked = source[None] == jnp.arange(owners, dtype=jnp.int32)[:, None, None]
    promoted = jnp.sum(jnp.where(picked[..., None, None], arrived, jnp.zeros_like(arrived)), axis=0)
    evicted = take_rows(cache, victim)
    leaving = take_rows(resident, victim) - owner_here * own_blocks
    slot_numbers = jnp.arange(slots, dtype=jnp.int32)
    block_numbers = jnp.arange(own_blocks, dtype=jnp.int32)
    new_cache = cache
    new_backing = backing
    for column in range(promoted_count):
        slot_hit = victim[:, column][:, None] == slot_numbers[None, :]
        new_cache = jnp.where(slot_hit[:, :, None, None], promoted[:, column][:, None], new_cache)
        block_hit = leaving[:, column][:, None] == block_numbers[None, :]
        new_backing = jnp.where(
            block_hit[:, :, None, None], evicted[:, column][:, None], new_backing
        )
    table = new_cache.reshape(held, slots * block, width)
    batches = lookups.shape[0]
    received = []
    for batch_turn in range(batches):
        pooled = pool_batch(lookups[batch_turn], route[batch_turn, 0], table)
        received.append(lax.all_to_all(pooled, "cache", split_axis=0, concat_axis=1, tiled=True))
    arrived_rows = jnp.stack(received)
    per_batch = arrived_rows.shape[1]
    features = arrived_rows.reshape(batches * per_batch, -1)
    low = jnp.dot(
        features,
        lax.all_gather(dcn_down, "cache", axis=0, tiled=True),
        preferred_element_type=jnp.float32,
    ).astype(jnp.bfloat16)
    gate = (
        jnp.dot(
            low,
            lax.all_gather(dcn_up, "cache", axis=1, tiled=True),
            preferred_element_type=jnp.float32,
        )
        + dcn_bias
    )
    crossed = (features * gate + features).astype(jnp.bfloat16)
    portion = mlp_in.shape[1] // lax.axis_size("owner")
    own_columns = lax.dynamic_slice_in_dim(mlp_in, owner_here * portion, portion, 1)
    column_block = lax.all_gather(own_columns, "cache", axis=0, tiled=True)
    before = jnp.dot(
        crossed,
        lax.all_gather(column_block, "owner", axis=1, tiled=True),
        preferred_element_type=jnp.float32,
    )
    hidden = jnp.maximum(before + mlp_bias, 0.0)
    scores = jnp.sum(hidden * mlp_out, axis=-1) + out_bias[0]
    return (scores.reshape(batches, 1, per_batch), new_cache, new_backing)


def solution(mesh):
    in_specs = (
        P("cache", None, None, None),
        P("cache", "owner", None, None),
        P("cache", None),
        P("cache", None),
        P("cache", None),
        P(None, "owner", "cache", None),
        P(None, "owner", None),
        P("cache", None),
        P(None, "cache"),
        P(),
        P("cache", None),
        P(),
        P(),
        P(),
    )
    out_specs = (
        P(None, "owner", "cache"),
        P("cache", None, None, None),
        P("cache", "owner", None, None),
    )
    return jax.shard_map(
        on_device, mesh=mesh, in_specs=in_specs, out_specs=out_specs, check_vma=False
    )
```

profile of v0, /device:TPU:0, one launch (start us, length us, event | category | flops | bytes accessed | tf_op | source)
XLA Modules:
  0.0 392.6 jit_solution(9065323531690684591)
XLA Ops:
  11.4 2.2 gather_fusion.2
  15.8 70.4 %all-gather.12.cloned.1.call-done = bf16[8192,256]{1,0:T(8,128)(2,1)} async-done(((bf16[1024,256]{1,0:T(8,128)(2,1)}), bf16[8192,256]{1,0:T(8,128)(2,1)}) %all-gather.12.cloned.1.call-update) | async-done | bytes 4194320 | tf_op jit(solution)/shard_map/all_gather | solution.py:100
  88.1 7.9 %gather_fusion = s32[1024,4,8]{2,1,0:T(4,128)} fusion(s32[1024,4,8]{2,1,0:T(4,128)S(1)} %bitcast.100, s32[1024]{0:T(1024)S(1)} %broadcast_clamp_fusion.1), kind=kCustom, calls=%fused_computation | custom fusion | bytes 266240 | tf_op jit(solution)/shard_map/gather | solution.py:12
  98.0 10.9 %all-gather.6.cloned.1.call-done = bf16[16,2,128,256]{3,2,1,0:T(8,128)(2,1)} async-done(((bf16[4,2,128,256]{3,2,1,0:T(8,128)(2,1)}), bf16[16,2,128,256]{3,2,1,0:T(8,128)(2,1)}) %all-gather.6.cloned.1.call-update) | async-done | bytes 2097168 | tf_op jit(solution)/shard_map/all_gather | solution.py:56
  108.9 2.1 select_reduce_fusion
  113.7 27.7 %while.26 = (s32[]{:T(128)}, bf16[2,512,4,256]{3,1,0,2:T(8,128)(2,1)}, s32[2,512,4,8]{1,3,2,0:T(8,128)S(1)}, bf16[4,512,256]{2,1,0:T(8,128)(2,1)}, s32[]{:T(128)}) while((s32[]{:T(128)}, bf16[2,512,4,256]{3,1,0,2:T(8,128)(2,1)}, s32[2,512,4,8]{1,3,2,0:T(8,128)S(1)}, bf16[4,512,256]{2,1,0:T(8,128)(2,1)}, s32[]{:T(128)}) %tuple.91), condition=%wide.region_3.4_spmd.clone, body=%wide.region_1.3_spmd.clone.sunk | while | flops 561512448 | bytes 10814045 | solution.py:24
  114.2 11.7 %fusion.60 = bf16[512,4,512]{2,1,0:T(4,128)(2,1)S(1)} fusion(s32[512,4,8]{2,1,0:T(4,128)S(1)} %copy.164), kind=kLoop, calls=%fused_computation.9.clone.1 | loop fusion | flops 24117248 | bytes 2162688 | tf_op jit(solution)/shard_map/while/body/eval_jaxpr/reduce_sum | solution.py:18
  128.0 11.7 %fusion.60 = bf16[512,4,512]{2,1,0:T(4,128)(2,1)S(1)} fusion(s32[512,4,8]{2,1,0:T(4,128)S(1)} %copy.164), kind=kLoop, calls=%fused_computation.9.clone.1 | loop fusion | flops 24117248 | bytes 2162688 | tf_op jit(solution)/shard_map/while/body/eval_jaxpr/reduce_sum | solution.py:18
  141.5 4.5 %copy.115 = bf16[1024,4,256]{2,1,0:T(4,128)(2,1)} copy(bf16[1024,4,256]{2,0,1:T(8,128)(2,1)} %bitcast.12) | data formatting | bytes 4194304 | tf_op jit(solution)/shard_map/reshape | solution.py:25
  146.0 5.5 %all-to-all-start = ((bf16[1024,4,256]{2,1,0:T(4,128)(2,1)}), bf16[1024,4,256]{2,1,0:T(4,128)(2,1)}, u32[]{:S(2)}, u32[]{:S(2)}) async-start(bf16[1024,4,256]{2,1,0:T(4,128)(2,1)} %copy.115), calls=%async_computation | async-start | bytes 4194304 | tf_op jit(solution)/shard_map/all_to_all | solution.py:80
  152.3 7.9 %gather_fusion.1 = s32[1024,4,8]{2,1,0:T(4,128)} fusion(s32[1024,4,8]{2,1,0:T(4,128)S(1)} %bitcast.101, s32[1024]{0:T(1024)S(1)} %broadcast_clamp_fusion), kind=kCustom, calls=%fused_computation.1 | custom fusion | bytes 266240 | tf_op jit(solution)/shard_map/gather | solution.py:12
  163.6 27.7 %while.27 = (s32[]{:T(128)}, bf16[2,512,4,256]{3,1,0,2:T(8,128)(2,1)}, s32[2,512,4,8]{1,3,2,0:T(8,128)S(1)}, bf16[4,512,256]{2,1,0:T(8,128)(2,1)}, s32[]{:T(128)}) while((s32[]{:T(128)}, bf16[2,512,4,256]{3,1,0,2:T(8,128)(2,1)}, s32[2,512,4,8]{1,3,2,0:T(8,128)S(1)}, bf16[4,512,256]{2,1,0:T(8,128)(2,1)}, s32[]{:T(128)}) %tuple.92), condition=%wide.region_6.7_spmd.clone, body=%wide.region_4.6_spmd.clone.sunk | while | flops 561512448 | bytes 10814045 | solution.py:24
  164.0 11.7 %fusion.64 = bf16[512,4,512]{2,1,0:T(4,128)(2,1)S(1)} fusion(s32[512,4,8]{2,1,0:T(4,128)S(1)} %copy.166), kind=kLoop, calls=%fused_computation.18.clone.1 | loop fusion | flops 24117248 | bytes 2162688 | tf_op jit(solution)/shard_map/while/body/eval_jaxpr/reduce_sum | solution.py:18
  177.9 11.7 %fusion.64 = bf16[512,4,512]{2,1,0:T(4,128)(2,1)S(1)} fusion(s32[512,4,8]{2,1,0:T(4,128)S(1)} %copy.166), kind=kLoop, calls=%fused_computation.18.clone.1 | loop fusion | flops 24117248 | bytes 2162688 | tf_op jit(solution)/shard_map/while/body/eval_jaxpr/reduce_sum | solution.py:18
  191.3 4.6 %copy.122 = bf16[1024,4,256]{2,1,0:T(4,128)(2,1)} copy(bf16[1024,4,256]{2,0,1:T(8,128)(2,1)} %bitcast.20) | data formatting | bytes 4194304 | tf_op jit(solution)/shard_map/reshape | solution.py:25
  195.9 17.7 %all-to-all-done = bf16[1024,4,256]{2,1,0:T(4,128)(2,1)} async-done(((bf16[1024,4,256]{2,1,0:T(4,128)(2,1)}), bf16[1024,4,256]{2,1,0:T(4,128)(2,1)}, u32[]{:S(2)}, u32[]{:S(2)}) %all-to-all-start) | async-done | bytes 2097184 | tf_op jit(solution)/shard_map/all_to_all | solution.py:80
  213.6 4.6 %all-to-all-start.1 = ((bf16[1024,4,256]{2,1,0:T(4,128)(2,1)}), bf16[1024,4,256]{2,1,0:T(4,128)(2,1)}, u32[]{:S(2)}, u32[]{:S(2)}) async-start(bf16[1024,4,256]{2,1,0:T(4,128)(2,1)} %copy.122), calls=%async_computation.1 | async-start | bytes 4194304 | tf_op jit(solution)/shard_map/all_to_all | solution.py:80
  220.7 3.3 select_select_fusion
  227.4 53.9 %all-to-all-done.1 = bf16[1024,4,256]{2,1,0:T(4,128)(2,1)} async-done(((bf16[1024,4,256]{2,1,0:T(4,128)(2,1)}), bf16[1024,4,256]{2,1,0:T(4,128)(2,1)}, u32[]{:S(2)}, u32[]{:S(2)}) %all-to-all-start.1) | async-done | bytes 2097184 | tf_op jit(solution)/shard_map/all_to_all | solution.py:80
  285.3 2.4 copy.125
  287.7 6.3 %copy.142 = bf16[32,8,32,256]{3,1,2,0:T(8,128)(2,1)} copy(bf16[32,8,32,256]{3,2,1,0:T(8,128)(2,1)S(1)} %bitcast.99) | data formatting | bytes 8388608
  294.0 4.3 %convolution_convert_fusion = bf16[256,128]{1,0:T(8,128)(2,1)S(1)} fusion(bf16[256,8192]{1,0:T(8,128)(2,1)} %bitcast.97, bf16[8192,128]{1,0:T(8,128)(2,1)} %all-gather.8.cloned.1.call-done), kind=kOutput, calls=%fused_computation.35 | convolution fusion | flops 536903680 | bytes 6356992 | tf_op jit(solution)/shard_map/dot_general | solution.py:84
  298.3 74.4 %all-gather.14.cloned.1.call-done = bf16[8192,1024]{1,0:T(8,128)(2,1)} async-done(((bf16[8192,256]{1,0:T(8,128)(2,1)}), bf16[8192,1024]{1,0:T(8,128)(2,1)}) %all-gather.14.cloned.1.call-update) | async-done | bytes 16777232 | tf_op jit(solution)/shard_map/all_gather | solution.py:103
  372.7 12.8 %fusion.33 = f32[256]{0:T(256)S(1)} fusion(bf16[8192,1024]{1,0:T(8,128)(2,1)} %all-gather.14.cloned.1.call-done, bf16[256,128]{1,0:T(8,128)(2,1)S(1)} %convolution_convert_fusion, bf16[128,8192]{1,0:T(8,128)(2,1)} %all-gather.10.cloned.1.call-done, bf16[256,8192]{1,0:T(8,128)(2,1)} %bitcast.98, f32[8192]{0:T(1024)S(1)} %copy-done.12, ...), kind=kOutput, calls=%fused_computation.34 | convolution fusion | flops 4843372544 | bytes 23176192 | tf_op jit(solution)/shard_map/dot_general | solution.py:101
  (98 shorter events, 35.2 us)
Async XLA Ops:
  7.2 1.6 copy-start
  7.2 79.0 %all-gather.12.cloned.1.call-start = ((), (), s32[]{:S(2)}) async-start(), calls=%async_computation.5 | async-start | bytes 4718592 | tf_op jit(solution)/shard_map/all_gather | solution.py:100
  9.6 99.3 %all-gather.6.cloned.1.call-start = ((), (), s32[]{:S(2)}) async-start(), calls=%async_computation.2 | async-start | bytes 2621440 | tf_op jit(solution)/shard_map/all_gather | solution.py:56
  14.5 279.5 %all-gather.8.cloned.1.call-start = ((), (), s32[]{:S(2)}) async-start(), calls=%async_computation.3 | async-start | bytes 2359296 | tf_op jit(solution)/shard_map/all_gather | solution.py:86
  15.2 283.1 %all-gather.10.cloned.1.call-start = ((), (), s32[]{:S(2)}) async-start(), calls=%async_computation.4 | async-start | bytes 2359296 | tf_op jit(solution)/shard_map/all_gather | solution.py:92
  15.8 356.9 %all-gather.14.cloned.1.call-start = ((), (), s32[]{:S(2)}) async-start(), calls=%async_computation.6 | async-start | bytes 20971520 | tf_op jit(solution)/shard_map/all_gather | solution.py:103
  86.2 0.7 copy-start.9
  86.2 1.0 copy-start.8
  86.3 1.8 copy-start.10
  96.0 1.9 copy-start.11
  97.9 13.2 %copy-start.4 = (bf16[4,4,128,256]{3,2,1,0:T(8,128)(2,1)S(1)}, bf16[4,4,128,256]{3,2,1,0:T(8,128)(2,1)}, u32[]{:S(2)}) copy-start(bf16[4,4,128,256]{3,2,1,0:T(8,128)(2,1)} %param.18) | copy-start | bytes 3145732
  114.2 11.7 %copy-start.6 = (bf16[4,512,256]{2,1,0:T(8,128)(2,1)S(1)}, bf16[4,512,256]{2,1,0:T(8,128)(2,1)}, u32[]{:S(2)}) copy-start(bf16[4,512,256]{2,1,0:T(8,128)(2,1)} %get-tuple-element.305) | copy-start | bytes 3145732 | tf_op jit(solution)/shard_map/while
  128.0 11.7 %copy-start.6 = (bf16[4,512,256]{2,1,0:T(8,128)(2,1)S(1)}, bf16[4,512,256]{2,1,0:T(8,128)(2,1)}, u32[]{:S(2)}) copy-start(bf16[4,512,256]{2,1,0:T(8,128)(2,1)} %get-tuple-element.305) | copy-start | bytes 3145732 | tf_op jit(solution)/shard_map/while
  146.0 67.6 %all-to-all-start = ((bf16[1024,4,256]{2,1,0:T(4,128)(2,1)}), bf16[1024,4,256]{2,1,0:T(4,128)(2,1)}, u32[]{:S(2)}, u32[]{:S(2)}) async-start(bf16[1024,4,256]{2,1,0:T(4,128)(2,1)} %copy.115), calls=%async_computation | async-start | bytes 4194304 | tf_op jit(solution)/shard_map/all_to_all | solution.py:80
  164.0 11.7 %copy-start.7 = (bf16[4,512,256]{2,1,0:T(8,128)(2,1)S(1)}, bf16[4,512,256]{2,1,0:T(8,128)(2,1)}, u32[]{:S(2)}) copy-start(bf16[4,512,256]{2,1,0:T(8,128)(2,1)} %get-tuple-element.290) | copy-start | bytes 3145732 | tf_op jit(solution)/shard_map/while
  177.8 11.7 %copy-start.7 = (bf16[4,512,256]{2,1,0:T(8,128)(2,1)S(1)}, bf16[4,512,256]{2,1,0:T(8,128)(2,1)}, u32[]{:S(2)}) copy-start(bf16[4,512,256]{2,1,0:T(8,128)(2,1)} %get-tuple-element.290) | copy-start | bytes 3145732 | tf_op jit(solution)/shard_map/while
  195.9 23.1 %copy-start.5 = (bf16[4,4,128,256]{3,2,1,0:T(8,128)(2,1)S(1)}, bf16[4,4,128,256]{3,2,1,0:T(8,128)(2,1)}, u32[]{:S(2)}) copy-start(bf16[4,4,128,256]{3,2,1,0:T(8,128)(2,1)} %param.18) | copy-start | bytes 3145732
  195.9 23.7 %copy-start.2 = (s32[4,4]{1,0:T(4,128)S(1)}, s32[4,4]{1,0:T(4,128)}, u32[]{:S(2)}) copy-start(s32[4,4]{1,0:T(4,128)} %param.20) | copy-start | bytes 196
  213.6 67.7 %all-to-all-start.1 = ((bf16[1024,4,256]{2,1,0:T(4,128)(2,1)}), bf16[1024,4,256]{2,1,0:T(4,128)(2,1)}, u32[]{:S(2)}, u32[]{:S(2)}) async-start(bf16[1024,4,256]{2,1,0:T(4,128)(2,1)} %copy.122), calls=%async_computation.1 | async-start | bytes 4194304 | tf_op jit(solution)/shard_map/all_to_all | solution.py:80
  283.2 1.6 copy-start.3
  294.0 78.7 %copy-start.12 = (f32[8192]{0:T(1024)S(1)}, f32[8192]{0:T(1024)}, u32[]{:S(2)}) copy-start(f32[8192]{0:T(1024)} %param.27) | copy-start | bytes 98308
  294.0 78.7 %copy-start.13 = (f32[1024]{0:T(1024)S(1)}, f32[1024]{0:T(1024)}, u32[]{:S(2)}) copy-start(f32[1024]{0:T(1024)} %param.30) | copy-start | bytes 12292
  294.0 78.7 %copy-start.14 = (f32[1024]{0:T(1024)S(1)}, f32[1024]{0:T(1024)}, u32[]{:S(2)}) copy-start(f32[1024]{0:T(1024)} %param.29) | copy-start | bytes 12292
  372.7 13.3 %copy-start.1 = (bf16[1024,1024]{1,0:T(8,128)(2,1)S(1)}, bf16[1024,1024]{1,0:T(8,128)(2,1)}, u32[]{:S(2)}) copy-start(bf16[1024,1024]{1,0:T(8,128)(2,1)} %param.28) | copy-start | bytes 6291460
Sparse Core Ops, SparseCore 0:
  10.7 75.4 all-gather.11
  87.8 21.0 all-gather.5
  111.1 52.2 all-gather.7
  165.3 89.3 all-gather.9
  256.1 116.5 all-gather.13
where the time goes:
time: 393 us
  waiting for transfers between devices  229 us (58%)
  local copies, waits for them, and re-layouts  58.2 us (15%)
  other arithmetic  56.9 us (14%)
  matrix products  23.8 us (6%)
  between operations  14.7 us (4%)
  starting transfers between devices  10.3 us (3%)
    all_gather x1, waiting for transfers between devices, on_device(): lax.all_gather(column_block, 'owner', axis=1, tiled=True)  74.4 us
    all_to_all x2, waiting for transfers between devices, on_device(): lax.all_to_all(pooled, 'cache', split_axis=0, concat_axis=1, tiled=True)  71.6 us
    all_gather x1, waiting for transfers between devices, on_device(): column_block = lax.all_gather(own_columns, 'cache', axis=0, tiled=True)  70.4 us
    reduce_sum x4, other arithmetic, one_block(): jnp.sum((lookup_block[..., None] == codes).astype(jnp.bfloat16), axis=2)  46.9 us
    gather x2, local copies, waits for them, and re-layouts, pool_batch(): requests = requests[order]  15.9 us
    unnamed x31, local copies, waits for them, and re-layouts  15.5 us
    dot_general x1, matrix products, on_device(): jnp.dot(crossed, lax.all_gather(column_block, 'owner', axis=1, tiled=True...  12.8 us
    all_gather x1, waiting for transfers between devices, on_device(): arrived = lax.all_gather(outgoing, 'owner', axis=0, tiled=True)  10.9 us
  transfers between devices with their start and end apart: 7, of which 5 were waited for; matrix products, arithmetic and copies ran while one was open for 31% of the time, Pallas kernels for 0%

commit v1 on v0

--- a/solution.py
+++ b/solution.py
@@ -2,6 +2,16 @@
 import jax.numpy as jnp
 from jax import lax
 from jax.sharding import PartitionSpec as P
+
+
+def gather_by_hops(x, axis, d):
+    count = lax.axis_size(axis)
+    held, tiles = (x, [x])
+    for _ in range(count - 1):
+        held = lax.ppermute(held, axis, [(i, (i + 1) % count) for i in range(count)])
+        tiles.insert(0, held)
+    row_of_blocks = jnp.concatenate(tiles, axis=d)
+    return jnp.roll(row_of_blocks, (lax.axis_index(axis) + 1) * x.shape[d], axis=d)
 
 
 def take_rows(table, wanted):
@@ -97,7 +107,7 @@
     crossed = (features * gate + features).astype(jnp.bfloat16)
     portion = mlp_in.shape[1] // lax.axis_size("owner")
     own_columns = lax.dynamic_slice_in_dim(mlp_in, owner_here * portion, portion, 1)
-    column_block = lax.all_gather(own_columns, "cache", axis=0, tiled=True)
+    column_block = gather_by_hops(own_columns, "cache", 0)
     before = jnp.dot(
         crossed,
         lax.all_gather(column_block, "owner", axis=1, tiled=True),

time: 393 us -> 333 us (0.85)
  waiting for transfers between devices: 229 us -> 167 us
    ppermute x0 -> x7, waiting for transfers between devices: none -> 129 us  [gather_by_hops(): lax.ppermute(held, axis, [(i, (i + 1) % count) for i in range(count)])]
    all_gather x1, waiting for transfers between devices: 74.4 us -> 0.02 us  [on_device(): lax.all_gather(column_block, 'owner', axis=1, tiled=True)]
    all_gather x1 -> x0, waiting for transfers between devices: 70.4 us -> none  [on_device(): column_block = lax.all_gather(own_columns, 'cache', axis=0, tiled=True)]
    all_to_all x2, waiting for transfers between devices: 71.6 us -> 37.8 us  [on_device(): lax.all_to_all(pooled, 'cache', split_axis=0, concat_axis=1, tiled=True)]
    all_gather x1, waiting for transfers between devices: 10.9 us -> 0.02 us  [on_device(): arrived = lax.all_gather(outgoing, 'owner', axis=0, tiled=True)]
    unnamed x31 -> x44, local copies, waits for them, and re-layouts: 15.5 us -> 16.5 us
  transfers between devices with their start and end apart: 7 -> 13, of which waited for: 5 -> 9; matrix products, arithmetic and copies ran while one was open for 31% -> 35% of each run, Pallas kernels for 0% -> 0%
where the time goes in v1:
time: 333 us; the launch traced here: 332 us
  waiting for transfers between devices  167 us (50%)
  other arithmetic  56.9 us (17%)
  local copies, waits for them, and re-layouts  55.8 us (17%)
  matrix products  24.8 us (7%)
  between operations  14.8 us (4%)
  starting transfers between devices  12 us (4%)
    ppermute x7, waiting for transfers between devices, gather_by_hops(): lax.ppermute(held, axis, [(i, (i + 1) % count) for i in range(count)])  129 us
    reduce_sum x4, other arithmetic, one_block(): jnp.sum((lookup_block[..., None] == codes).astype(jnp.bfloat16), axis=2)  46.9 us
    all_to_all x2, waiting for transfers between devices, on_device(): lax.all_to_all(pooled, 'cache', split_axis=0, concat_axis=1, tiled=True)  37.8 us
    unnamed x44, local copies, waits for them, and re-layouts  16.5 us
    gather x2, local copies, waits for them, and re-layouts, pool_batch(): requests = requests[order]  15.8 us
    dot_general x1, matrix products, on_device(): jnp.dot(crossed, lax.all_gather(column_block, 'owner', axis=1, tiled=True...  12.7 us
    all_to_all x2, starting transfers between devices, on_device(): lax.all_to_all(pooled, 'cache', split_axis=0, concat_axis=1, tiled=True)  8.83 us
    dot_general x4, matrix products, one_block(): jnp.einsum('rfk,fke->rfe', counts, table, preferred_element_type=jnp.floa...  7.99 us
  transfers between devices with their start and end apart: 13, of which 9 were waited for; matrix products, arithmetic and copies ran while one was open for 35% of the time, Pallas kernels for 0%

profile of v1, /device:TPU:0, one launch (start us, length us, event | category | flops | bytes accessed | tf_op | source)
XLA Modules:
  0.0 332.1 jit_solution(14820557727270067764)
XLA Ops:
  13.9 3.0 collective-permute-start
  16.9 15.0 %collective-permute-done = bf16[1024,256]{1,0:T(8,128)(2,1)S(1)} collective-permute-done((bf16[1024,256]{1,0:T(8,128)(2,1)S(1)}, bf16[1024,256]{1,0:T(8,128)(2,1)S(1)}, u32[]{:S(2)}, u32[]{:S(2)}) %collective-permute-start) | collective-permute-done | bytes 524320 | tf_op jit(solution)/shard_map/ppermute | solution.py:11
  31.9 15.8 %collective-permute-done.1 = bf16[1024,256]{1,0:T(8,128)(2,1)S(1)} collective-permute-done((bf16[1024,256]{1,0:T(8,128)(2,1)S(1)}, bf16[1024,256]{1,0:T(8,128)(2,1)S(1)}, u32[]{:S(2)}, u32[]{:S(2)}) %collective-permute-start.1) | collective-permute-done | bytes 524320 | tf_op jit(solution)/shard_map/ppermute | solution.py:11
  47.7 23.4 %collective-permute-done.2 = bf16[1024,256]{1,0:T(8,128)(2,1)S(1)} collective-permute-done((bf16[1024,256]{1,0:T(8,128)(2,1)S(1)}, bf16[1024,256]{1,0:T(8,128)(2,1)S(1)}, u32[]{:S(2)}, u32[]{:S(2)}) %collective-permute-start.2) | collective-permute-done | bytes 524320 | tf_op jit(solution)/shard_map/ppermute | solution.py:11
  71.0 25.8 %collective-permute-done.3 = bf16[1024,256]{1,0:T(8,128)(2,1)S(1)} collective-permute-done((bf16[1024,256]{1,0:T(8,128)(2,1)S(1)}, bf16[1024,256]{1,0:T(8,128)(2,1)S(1)}, u32[]{:S(2)}, u32[]{:S(2)}) %collective-permute-start.3) | collective-permute-done | bytes 524320 | tf_op jit(solution)/shard_map/ppermute | solution.py:11
  96.8 16.1 %collective-permute-done.4 = bf16[1024,256]{1,0:T(8,128)(2,1)S(1)} collective-permute-done((bf16[1024,256]{1,0:T(8,128)(2,1)S(1)}, bf16[1024,256]{1,0:T(8,128)(2,1)S(1)}, u32[]{:S(2)}, u32[]{:S(2)}) %collective-permute-start.4) | collective-permute-done | bytes 524320 | tf_op jit(solution)/shard_map/ppermute | solution.py:11
  113.0 12.6 %collective-permute-done.5 = bf16[1024,256]{1,0:T(8,128)(2,1)S(1)} collective-permute-done((bf16[1024,256]{1,0:T(8,128)(2,1)S(1)}, bf16[1024,256]{1,0:T(8,128)(2,1)S(1)}, u32[]{:S(2)}, u32[]{:S(2)}) %collective-permute-start.5) | collective-permute-done | bytes 524320 | tf_op jit(solution)/shard_map/ppermute | solution.py:11
  125.6 20.3 %collective-permute-done.6 = bf16[1024,256]{1,0:T(8,128)(2,1)} collective-permute-done((bf16[1024,256]{1,0:T(8,128)(2,1)S(1)}, bf16[1024,256]{1,0:T(8,128)(2,1)}, u32[]{:S(2)}, u32[]{:S(2)}) %collective-permute-start.6) | collective-permute-done | bytes 524320 | tf_op jit(solution)/shard_map/ppermute | solution.py:11
  152.9 7.9 %gather_fusion = s32[1024,4,8]{2,1,0:T(4,128)} fusion(s32[1024,4,8]{2,1,0:T(4,128)S(1)} %bitcast.100, s32[1024]{0:T(1024)S(1)} %get-tuple-element.224), kind=kCustom, calls=%fused_computation | custom fusion | bytes 266240 | tf_op jit(solution)/shard_map/gather | solution.py:22
  166.3 28.4 %while.26 = (s32[]{:T(128)}, bf16[2,512,4,256]{3,1,0,2:T(8,128)(2,1)S(1)}, s32[2,512,4,8]{1,3,2,0:T(8,128)S(1)}, bf16[4,512,256]{2,1,0:T(8,128)(2,1)}, s32[]{:T(128)}) while((s32[]{:T(128)}, bf16[2,512,4,256]{3,1,0,2:T(8,128)(2,1)S(1)}, s32[2,512,4,8]{1,3,2,0:T(8,128)S(1)}, bf16[4,512,256]{2,1,0:T(8,128)(2,1)}, s32[]{:T(128)}) %tuple.90), condition=%wide.region_3.4_spmd.clone, body=%wide.region_1.3_spmd.clone.sunk | while | flops 561512448 | bytes 6619205 | solution.py:34
  166.8 11.7 %fusion.60 = bf16[512,4,512]{2,1,0:T(4,128)(2,1)S(1)} fusion(s32[512,4,8]{2,1,0:T(4,128)S(1)} %copy.164), kind=kLoop, calls=%fused_computation.9.clone.1 | loop fusion | flops 24117248 | bytes 2162688 | tf_op jit(solution)/shard_map/while/body/eval_jaxpr/reduce_sum | solution.py:28
  181.1 11.7 %fusion.60 = bf16[512,4,512]{2,1,0:T(4,128)(2,1)S(1)} fusion(s32[512,4,8]{2,1,0:T(4,128)S(1)} %copy.164), kind=kLoop, calls=%fused_computation.9.clone.1 | loop fusion | flops 24117248 | bytes 2162688 | tf_op jit(solution)/shard_map/while/body/eval_jaxpr/reduce_sum | solution.py:28
  197.7 4.5 %all-to-all-start = ((bf16[1024,4,256]{2,1,0:T(4,128)(2,1)}), bf16[1024,4,256]{2,1,0:T(4,128)(2,1)}, u32[]{:S(2)}, u32[]{:S(2)}) async-start(bf16[1024,4,256]{2,1,0:T(4,128)(2,1)} %copy.115), calls=%async_computation | async-start | bytes 4194304 | tf_op jit(solution)/shard_map/all_to_all | solution.py:90
  203.1 7.9 %gather_fusion.1 = s32[1024,4,8]{2,1,0:T(4,128)} fusion(s32[1024,4,8]{2,1,0:T(4,128)S(1)} %bitcast.101, s32[1024]{0:T(1024)S(1)} %get-tuple-element.223), kind=kCustom, calls=%fused_computation.1 | custom fusion | bytes 266240 | tf_op jit(solution)/shard_map/gather | solution.py:22
  213.0 28.2 %while.27 = (s32[]{:T(128)}, bf16[2,512,4,256]{3,1,0,2:T(8,128)(2,1)S(1)}, s32[2,512,4,8]{1,3,2,0:T(8,128)S(1)}, bf16[4,512,256]{2,1,0:T(8,128)(2,1)}, s32[]{:T(128)}) while((s32[]{:T(128)}, bf16[2,512,4,256]{3,1,0,2:T(8,128)(2,1)S(1)}, s32[2,512,4,8]{1,3,2,0:T(8,128)S(1)}, bf16[4,512,256]{2,1,0:T(8,128)(2,1)}, s32[]{:T(128)}) %tuple.91), condition=%wide.region_6.7_spmd.clone, body=%wide.region_4.6_spmd.clone.sunk | while | flops 561512448 | bytes 6619205 | solution.py:34
  213.4 11.7 %fusion.64 = bf16[512,4,512]{2,1,0:T(4,128)(2,1)S(1)} fusion(s32[512,4,8]{2,1,0:T(4,128)S(1)} %copy.166), kind=kLoop, calls=%fused_computation.18.clone.1 | loop fusion | flops 24117248 | bytes 2162688 | tf_op jit(solution)/shard_map/while/body/eval_jaxpr/reduce_sum | solution.py:28
  227.5 11.7 %fusion.64 = bf16[512,4,512]{2,1,0:T(4,128)(2,1)S(1)} fusion(s32[512,4,8]{2,1,0:T(4,128)S(1)} %copy.166), kind=kLoop, calls=%fused_computation.18.clone.1 | loop fusion | flops 24117248 | bytes 2162688 | tf_op jit(solution)/shard_map/while/body/eval_jaxpr/reduce_sum | solution.py:28
  241.2 3.0 copy.122
  245.6 4.3 %all-to-all-start.1 = ((bf16[1024,4,256]{2,1,0:T(4,128)(2,1)}), bf16[1024,4,256]{2,1,0:T(4,128)(2,1)S(1)}, u32[]{:S(2)}, u32[]{:S(2)}) async-start(bf16[1024,4,256]{2,1,0:T(4,128)(2,1)} %copy.122), calls=%async_computation.1 | async-start | bytes 4194304 | tf_op jit(solution)/shard_map/all_to_all | solution.py:90
  254.2 3.3 select_select_fusion
  260.9 36.4 %all-to-all-done.1 = bf16[1024,4,256]{2,1,0:T(4,128)(2,1)S(1)} async-done(((bf16[1024,4,256]{2,1,0:T(4,128)(2,1)}), bf16[1024,4,256]{2,1,0:T(4,128)(2,1)S(1)}, u32[]{:S(2)}, u32[]{:S(2)}) %all-to-all-start.1) | async-done | bytes 2097184 | tf_op jit(solution)/shard_map/all_to_all | solution.py:90
  301.7 6.3 %copy.142 = bf16[32,8,32,256]{3,1,2,0:T(8,128)(2,1)} copy(bf16[32,8,32,256]{3,2,1,0:T(8,128)(2,1)S(1)} %bitcast.99) | data formatting | bytes 8388608
  308.0 4.1 %convolution_convert_fusion = bf16[256,128]{1,0:T(8,128)(2,1)S(1)} fusion(bf16[256,8192]{1,0:T(8,128)(2,1)} %bitcast.97, bf16[8192,128]{1,0:T(8,128)(2,1)} %all-gather.7.cloned.1.call-done), kind=kOutput, calls=%fused_computation.35 | convolution fusion | flops 536903680 | bytes 6356992 | tf_op jit(solution)/shard_map/dot_general | solution.py:94
  312.3 12.7 %fusion.33 = f32[256]{0:T(256)S(1)} fusion(bf16[8192,1024]{1,0:T(8,128)(2,1)} %all-gather.11.cloned.1.call-done, bf16[256,128]{1,0:T(8,128)(2,1)S(1)} %convolution_convert_fusion, bf16[128,8192]{1,0:T(8,128)(2,1)} %all-gather.9.cloned.1.call-done, bf16[256,8192]{1,0:T(8,128)(2,1)} %bitcast.98, f32[8192]{0:T(1024)S(1)} %copy-done.9, ...), kind=kOutput, calls=%fused_computation.34 | convolution fusion | flops 4843372544 | bytes 23176192 | tf_op jit(solution)/shard_map/dot_general | solution.py:111
  (115 shorter events, 47.9 us)
Async XLA Ops:
  7.2 245.0 %copy-start = (s32[4,4]{1,0:T(4,128)S(1)}, s32[4,4]{1,0:T(4,128)}, u32[]{:S(2)}) copy-start(s32[4,4]{1,0:T(4,128)} %param.20) | copy-start | bytes 196
  7.2 155.6 %all-gather.5.cloned.1.call-start = ((), (), s32[]{:S(2)}) async-start(), calls=%async_computation.2 | async-start | bytes 2621440 | tf_op jit(solution)/shard_map/all_gather | solution.py:66
  12.0 296.0 %all-gather.7.cloned.1.call-start = ((), (), s32[]{:S(2)}) async-start(), calls=%async_computation.3 | async-start | bytes 2359296 | tf_op jit(solution)/shard_map/all_gather | solution.py:96
  12.8 299.4 %all-gather.9.cloned.1.call-start = ((), (), s32[]{:S(2)}) async-start(), calls=%async_computation.4 | async-start | bytes 2359296 | tf_op jit(solution)/shard_map/all_gather | solution.py:102
  13.9 18.0 %collective-permute-start = (bf16[1024,256]{1,0:T(8,128)(2,1)S(1)}, bf16[1024,256]{1,0:T(8,128)(2,1)S(1)}, u32[]{:S(2)}, u32[]{:S(2)}) collective-permute-start(bf16[1024,256]{1,0:T(8,128)(2,1)S(1)} %constant_dynamic-slice_fusion.1), channel_id=1, source_target_pairs={{0,4},{4,8},{8,12},{12,16},{16,20},{20,24},{24,28},{28,0},{1,5},{5... | collective-permute-start | bytes 1572872 | tf_op jit(solution)/shard_map/ppermute | solution.py:11
  31.9 15.8 %collective-permute-start.1 = (bf16[1024,256]{1,0:T(8,128)(2,1)S(1)}, bf16[1024,256]{1,0:T(8,128)(2,1)S(1)}, u32[]{:S(2)}, u32[]{:S(2)}) collective-permute-start(bf16[1024,256]{1,0:T(8,128)(2,1)S(1)} %collective-permute-done), channel_id=1, source_target_pairs={{0,4},{4,8},{8,12},{12,16},{16,20},{20,24},{24,28},{28,0},{1,5},{5... | collective-permute-start | bytes 1572872 | tf_op jit(solution)/shard_map/ppermute | solution.py:11
  47.7 23.4 %collective-permute-start.2 = (bf16[1024,256]{1,0:T(8,128)(2,1)S(1)}, bf16[1024,256]{1,0:T(8,128)(2,1)S(1)}, u32[]{:S(2)}, u32[]{:S(2)}) collective-permute-start(bf16[1024,256]{1,0:T(8,128)(2,1)S(1)} %collective-permute-done.1), channel_id=1, source_target_pairs={{0,4},{4,8},{8,12},{12,16},{16,20},{20,24},{24,28},{28,0},{1,5},{5... | collective-permute-start | bytes 1572872 | tf_op jit(solution)/shard_map/ppermute | solution.py:11
  71.0 25.8 %collective-permute-start.3 = (bf16[1024,256]{1,0:T(8,128)(2,1)S(1)}, bf16[1024,256]{1,0:T(8,128)(2,1)S(1)}, u32[]{:S(2)}, u32[]{:S(2)}) collective-permute-start(bf16[1024,256]{1,0:T(8,128)(2,1)S(1)} %collective-permute-done.2), channel_id=1, source_target_pairs={{0,4},{4,8},{8,12},{12,16},{16,20},{20,24},{24,28},{28,0},{1,5},{5... | collective-permute-start | bytes 1572872 | tf_op jit(solution)/shard_map/ppermute | solution.py:11
  96.8 16.1 %collective-permute-start.4 = (bf16[1024,256]{1,0:T(8,128)(2,1)S(1)}, bf16[1024,256]{1,0:T(8,128)(2,1)S(1)}, u32[]{:S(2)}, u32[]{:S(2)}) collective-permute-start(bf16[1024,256]{1,0:T(8,128)(2,1)S(1)} %collective-permute-done.3), channel_id=1, source_target_pairs={{0,4},{4,8},{8,12},{12,16},{16,20},{20,24},{24,28},{28,0},{1,5},{5... | collective-permute-start | bytes 1572872 | tf_op jit(solution)/shard_map/ppermute | solution.py:11
  112.9 12.6 %collective-permute-start.5 = (bf16[1024,256]{1,0:T(8,128)(2,1)S(1)}, bf16[1024,256]{1,0:T(8,128)(2,1)S(1)}, u32[]{:S(2)}, u32[]{:S(2)}) collective-permute-start(bf16[1024,256]{1,0:T(8,128)(2,1)S(1)} %collective-permute-done.4), channel_id=1, source_target_pairs={{0,4},{4,8},{8,12},{12,16},{16,20},{20,24},{24,28},{28,0},{1,5},{5... | collective-permute-start | bytes 1572872 | tf_op jit(solution)/shard_map/ppermute | solution.py:11
  113.0 199.3 %all-gather.11.cloned.1.call-start = ((), (), s32[]{:S(2)}) async-start(), calls=%async_computation.5 | async-start | bytes 20971520 | tf_op jit(solution)/shard_map/all_gather | solution.py:113
  125.6 20.3 %collective-permute-start.6 = (bf16[1024,256]{1,0:T(8,128)(2,1)S(1)}, bf16[1024,256]{1,0:T(8,128)(2,1)}, u32[]{:S(2)}, u32[]{:S(2)}) collective-permute-start(bf16[1024,256]{1,0:T(8,128)(2,1)S(1)} %collective-permute-done.5), channel_id=1, source_target_pairs={{0,4},{4,8},{8,12},{12,16},{16,20},{20,24},{24,28},{28,0},{1,5},{5... | collective-permute-start | bytes 1572872 | tf_op jit(solution)/shard_map/ppermute | solution.py:11
  125.6 21.6 %copy-start.4 = (bf16[1024,1024]{1,0:T(8,128)(2,1)S(1)}, bf16[1024,1024]{1,0:T(8,128)(2,1)}, u32[]{:S(2)}) copy-start(bf16[1024,1024]{1,0:T(8,128)(2,1)} %param.28) | copy-start | bytes 6291460
  151.0 1.0 copy-start.5
  151.0 1.8 copy-start.7
  152.0 10.7 %copy-start.8 = (s32[4,2]{0,1:T(2,128)S(1)}, s32[4,2]{0,1:T(2,128)}, u32[]{:S(2)}) copy-start(s32[4,2]{0,1:T(2,128)} %param.22) | copy-start | bytes 100
  152.9 12.1 %copy-start.2 = (bf16[4,4,128,256]{3,2,1,0:T(8,128)(2,1)S(1)}, bf16[4,4,128,256]{3,2,1,0:T(8,128)(2,1)}, u32[]{:S(2)}) copy-start(bf16[4,4,128,256]{3,2,1,0:T(8,128)(2,1)} %param.18) | copy-start | bytes 3145732
  197.7 47.9 %all-to-all-start = ((bf16[1024,4,256]{2,1,0:T(4,128)(2,1)}), bf16[1024,4,256]{2,1,0:T(4,128)(2,1)}, u32[]{:S(2)}, u32[]{:S(2)}) async-start(bf16[1024,4,256]{2,1,0:T(4,128)(2,1)} %copy.115), calls=%async_computation | async-start | bytes 4194304 | tf_op jit(solution)/shard_map/all_to_all | solution.py:90
  241.2 9.5 %copy-start.3 = (bf16[4,4,128,256]{3,2,1,0:T(8,128)(2,1)S(1)}, bf16[4,4,128,256]{3,2,1,0:T(8,128)(2,1)}, u32[]{:S(2)}) copy-start(bf16[4,4,128,256]{3,2,1,0:T(8,128)(2,1)} %param.18) | copy-start | bytes 3145732
  245.6 51.7 %all-to-all-start.1 = ((bf16[1024,4,256]{2,1,0:T(4,128)(2,1)}), bf16[1024,4,256]{2,1,0:T(4,128)(2,1)S(1)}, u32[]{:S(2)}, u32[]{:S(2)}) async-start(bf16[1024,4,256]{2,1,0:T(4,128)(2,1)} %copy.122), calls=%async_computation.1 | async-start | bytes 4194304 | tf_op jit(solution)/shard_map/all_to_all | solution.py:90
  297.3 1.6 copy-start.1
  308.0 4.2 %copy-start.9 = (f32[8192]{0:T(1024)S(1)}, f32[8192]{0:T(1024)}, u32[]{:S(2)}) copy-start(f32[8192]{0:T(1024)} %param.27) | copy-start | bytes 98308
  308.0 4.2 %copy-start.10 = (f32[1024]{0:T(1024)S(1)}, f32[1024]{0:T(1024)}, u32[]{:S(2)}) copy-start(f32[1024]{0:T(1024)} %param.30) | copy-start | bytes 12292
  308.0 4.2 %copy-start.11 = (f32[1024]{0:T(1024)S(1)}, f32[1024]{0:T(1024)}, u32[]{:S(2)}) copy-start(f32[1024]{0:T(1024)} %param.29) | copy-start | bytes 12292
  (1 other events, 0.7 us)
Sparse Core Ops, SparseCore 0:
  12.1 25.2 all-gather.4
  39.6 65.4 all-gather.6
  113.1 56.9 all-gather.8
  171.5 106.6 all-gather.10
